TPU v7x, 32 devices: a whole 2x2x4 slice. The times are simulated.
32 devices in a mesh: groups: 2 (over y), wide: 8 (over z, x), narrow: 2 (over core).
Axes of the slice: x: 2, y: 2, z: 4, core: 2. Of those that a mesh axis runs over, the one named last changes fastest.
Arguments:
- pieces: bfloat16 [2, 1024, 8192], P(None, ('groups', 'wide'), 'narrow'), parts along dimension 1, may hold values from -6 to 6
- destination: int32 [512], P('wide'), may hold values from 0 to 511, as said below
- first_offset: int32 [512], P('wide'), may hold values from 0 to 6144, as said below
- valid_length: int32 [512], P('wide'), may hold values from 2048 to 8192
- midpoint_factor: float32 [1024, 128], P(('groups', 'wide')), parts along dimension 0, may hold values from -0.3 to 0.3
- offset_factor: float32 [16384, 128], P(('groups', 'narrow')), parts along dimension 0, may hold values from -6 to 6
- threshold: float32 [16384], P(('groups', 'narrow')), parts along dimension 0, may hold values from 0.3 to 3
Outputs:
- sparse: bfloat16 [2, 1024, 8192], P(None, ('groups', 'wide'), 'narrow'), parts along dimension 1
- new_midpoint: float32 [1024, 128], P(('groups', 'wide')), parts along dimension 0
- new_offset: float32 [16384, 128], P(('groups', 'narrow')), parts along dimension 0
There are 2 independent parts, one for each index of `groups`. A program takes and returns all parts, laid end to end along the dimension named above; an argument that names none is the same for every part. Nothing has to cross between parts.
Inputs may be any that keep to these rules, and one draw needn't show every extreme that they name: destination is a permutation of the midpoint rows; the 64 segments of one device (aligned blocks) name at most 16 rows of any aligned block of 64 midpoint rows, and exactly 16 rows of some block. first_offset + valid_length <= 8192.
All inputs are finite; a program needn't handle non-finite values.
Results may differ from a plain program's by a relative error of at most 0.005.
Values may be sent and summed in bfloat16 or wider, within the bound.
No kernel may reach another device: no remote copies, remote signals or barrier semaphores. Data moves between devices by JAX's collectives and lax.ppermute only.
A program may use at most 64 MiB of HBM per device.

v0:
```python
import jax
import jax.numpy as jnp
from jax import lax
from jax.sharding import PartitionSpec as P

ITERS = 2


epsilon = 1e-06


def refine(observed, inside, row_factor, left_factor, right_factor, threshold):
    half_rank = right_factor.shape[1] // 2
    right_low = right_factor.astype(jnp.bfloat16)
    right_turn = jnp.concatenate(
        [-right_factor[:, half_rank:], right_factor[:, :half_rank]], 1
    ).astype(jnp.bfloat16)
    row_turn = jnp.concatenate([row_factor[:, half_rank:], -row_factor[:, :half_rank]], 1)
    model_real = jnp.dot(row_factor, right_low.T, preferred_element_type=jnp.float32)
    model_imag = jnp.dot(row_factor, right_turn.T, preferred_element_type=jnp.float32)
    resid_real = jnp.where(inside, observed[0].astype(jnp.float32) - model_real, jnp.float32(0.0))
    resid_imag = jnp.where(inside, observed[1].astype(jnp.float32) - model_imag, jnp.float32(0.0))
    magnitude = jnp.sqrt(resid_real * resid_real + resid_imag * resid_imag)
    factor = jnp.maximum(magnitude - threshold[None, :], 0.0) / jnp.maximum(
        magnitude, threshold[None, :]
    )
    sparse_real = resid_real * factor
    sparse_imag = resid_imag * factor
    error_real = (resid_real - sparse_real).astype(jnp.bfloat16)
    error_imag = (resid_imag - sparse_imag).astype(jnp.bfloat16)
    row_grad = jnp.dot(error_real, right_low, preferred_element_type=jnp.float32) + jnp.dot(
        error_imag, right_turn, preferred_element_type=jnp.float32
    )
    right_norm = jnp.sum(right_factor[:, :half_rank] ** 2 + right_factor[:, half_rank:] ** 2, 0)
    row_grad, right_norm = lax.psum((row_grad, right_norm), "narrow")
    row_step = row_grad / (jnp.concatenate([right_norm, right_norm]) + epsilon)
    offset_grad = jnp.dot(error_real.T, row_factor, preferred_element_type=jnp.float32) + jnp.dot(
        error_imag.T, row_turn, preferred_element_type=jnp.float32
    )
    left_norm = jnp.sum(left_factor[:, :half_rank] ** 2 + left_factor[:, half_rank:] ** 2, 0)
    offset_grad, left_norm = lax.psum((offset_grad, left_norm), "wide")
    right_next = right_factor + offset_grad / (jnp.concatenate([left_norm, left_norm]) + epsilon)
    return (jnp.stack([sparse_real, sparse_imag]), row_step, right_next)


def local(
    pieces, destination, first_offset, valid_length, midpoint_factor, offset_factor, threshold
):
    row_count = destination.shape[0]
    wide_count = lax.axis_size("wide")
    capacity = 2 * row_count // wide_count
    slot_count = wide_count * capacity
    owner_dev = destination // row_count
    row_in = destination % row_count
    one_hot = (owner_dev[:, None] == jnp.arange(wide_count, dtype=jnp.int32)[None, :]).astype(
        jnp.int32
    )
    before = jnp.cumsum(one_hot, 0) - one_hot
    rank_in = jnp.sum(before * one_hot, 1)
    send_slot = owner_dev * capacity + rank_in
    source_row = (
        jnp.zeros((slot_count,), jnp.int32)
        .at[send_slot]
        .set(jnp.arange(row_count, dtype=jnp.int32))
    )
    filled = jnp.zeros((slot_count,), jnp.bool_).at[send_slot].set(True)
    col_count = pieces.shape[2]
    columns = lax.axis_index("narrow") * col_count + jnp.arange(col_count, dtype=jnp.int32)
    left_factor = midpoint_factor
    right_factor = offset_factor
    request = jnp.where(filled, row_in[source_row], row_count)
    asked_rows = lax.all_to_all(request, "wide", split_axis=0, concat_axis=0, tiled=True)
    asked_valid = asked_rows < row_count
    safe_rows = jnp.minimum(asked_rows, row_count - 1)
    landing = (
        jnp.zeros((row_count,), jnp.int32)
        .at[asked_rows]
        .set(jnp.arange(slot_count, dtype=jnp.int32), mode="drop")
    )
    inside = (columns[None, :] >= first_offset[:, None]) & (
        columns[None, :] < (first_offset + valid_length)[:, None]
    )
    for sweep in range(ITERS):
        answer = jnp.where(
            asked_valid[:, None],
            jnp.take(left_factor.astype(jnp.bfloat16), safe_rows, axis=0),
            jnp.zeros((), jnp.bfloat16),
        )
        fetched = lax.all_to_all(answer, "wide", split_axis=0, concat_axis=0, tiled=True)
        row_factor = jnp.take(fetched, send_slot, axis=0)
        sparse, row_step, right_factor = refine(
            pieces, inside, row_factor, left_factor, right_factor, threshold
        )
        outgoing = jnp.where(
            filled[:, None], jnp.take(row_step, source_row, axis=0), jnp.float32(0.0)
        )
        arriving = lax.all_to_all(
            outgoing.astype(jnp.bfloat16), "wide", split_axis=0, concat_axis=0, tiled=True
        ).astype(outgoing.dtype)
        left_factor = left_factor + jnp.take(arriving, landing, axis=0)
    result = sparse.astype(jnp.bfloat16)
    return (result, left_factor, right_factor)


def solution(mesh):
    placed = (
        P(None, ("groups", "wide"), "narrow"),
        P("wide"),
        P("wide"),
        P("wide"),
        P(("groups", "wide"), None),
        P(("groups", "narrow"), None),
        P(("groups", "narrow")),
    )
    return jax.shard_map(
        local,
        mesh=mesh,
        in_specs=placed,
        out_specs=(
            P(None, ("groups", "wide"), "narrow"),
            P(("groups", "wide"), None),
            P(("groups", "narrow"), None),
        ),
        check_vma=False,
    )
```

profile of v0, /device:TPU:0, one launch (start us, length us, event | category | flops | bytes accessed | tf_op | source)
XLA Modules:
  0.0 269.3 jit_solution(9825216113704867588)
XLA Ops:
  8.2 0.8 scatter_custom_fusion.1
  9.0 0.8 scatter_custom_fusion
  9.8 1.2 gather_fusion
  11.7 7.3 %all-to-all-start = ((s32[8,16,1]{1,2,0:T(1,128)}), s32[8,16,1]{1,2,0:T(1,128)S(1)}, u32[]{:S(2)}, u32[]{:S(2)}) async-start(s32[8,16,1]{1,2,0:T(1,128)} %bitcast.1), calls=%async_computation | async-start | bytes 8192 | tf_op jit(solution)/shard_map/all_to_all | solution.py:72
  19.1 4.0 %add_reduce_fusion.1 = (f32[64]{0:T(128)S(1)}, bf16[4096,64]{1,0:T(8,128)(2,1)}) fusion(f32[4096,128]{1,0:T(8,128)} %param.20), kind=kLoop, calls=%fused_computation.26 | loop fusion | flops 1572800 | bytes 2621696 | tf_op jit(solution)/shard_map/reduce_sum | solution.py:34
  23.8 1.6 all-to-all-done
  28.3 4.4 %all-to-all-start.1 = ((bf16[8,16,128]{2,1,0:T(8,128)(2,1)}), bf16[8,16,128]{2,1,0:T(8,128)(2,1)S(1)}, u32[]{:S(2)}, u32[]{:S(2)}) async-start(bf16[8,16,128]{2,1,0:T(8,128)(2,1)} %bitcast.4), calls=%async_computation.1 | async-start | bytes 65536 | tf_op jit(solution)/shard_map/all_to_all | solution.py:89
  32.8 1.0 scatter_custom_fusion.2
  33.8 5.5 %all-to-all-done.1 = bf16[8,16,128]{2,1,0:T(8,128)(2,1)S(1)} async-done(((bf16[8,16,128]{2,1,0:T(8,128)(2,1)}), bf16[8,16,128]{2,1,0:T(8,128)(2,1)S(1)}, u32[]{:S(2)}, u32[]{:S(2)}) %all-to-all-start.1) | async-done | bytes 32800 | tf_op jit(solution)/shard_map/all_to_all | solution.py:89
  40.1 1.7 fusion.3
  41.8 1.5 fusion.5
  44.2 1.8 convolution_add_fusion.1
  46.1 2.1 convolution_add_fusion.3
  48.2 3.5 %all-reduce.2 = (f32[64,128]{1,0:T(8,128)S(1)}, f32[64]{0:T(128)S(1)}) all-reduce(f32[64,128]{1,0:T(8,128)S(1)} %convolution_add_fusion.3, f32[64]{0:T(128)S(1)} %get-tuple-element.27), channel_id=1, replica_groups=mesh['groups'=2,'wide'=8,'narrow'=2] {'narrow'}, use_global_device_ids=true, to_apply=%region_4.7 | all-reduce | flops 8256 | bytes 66048 | tf_op jit(solution)/shard_map/psum | solution.py:35
  53.2 3.3 %all-to-all-start.2 = ((bf16[8,16,128]{2,1,0:T(8,128)(2,1)}), bf16[8,16,128]{2,1,0:T(8,128)(2,1)S(1)}, u32[]{:S(2)}, u32[]{:S(2)}) async-start(bf16[8,16,128]{2,1,0:T(8,128)(2,1)} %bitcast.7), calls=%async_computation.2 | async-start | bytes 65536 | tf_op jit(solution)/shard_map/all_to_all | solution.py:97
  56.5 7.1 %all-to-all-done.2 = bf16[8,16,128]{2,1,0:T(8,128)(2,1)S(1)} async-done(((bf16[8,16,128]{2,1,0:T(8,128)(2,1)}), bf16[8,16,128]{2,1,0:T(8,128)(2,1)S(1)}, u32[]{:S(2)}, u32[]{:S(2)}) %all-to-all-start.2) | async-done | bytes 32800 | tf_op jit(solution)/shard_map/all_to_all | solution.py:97
  65.8 3.3 %all-to-all-start.3 = ((bf16[8,16,128]{2,1,0:T(8,128)(2,1)}), bf16[8,16,128]{2,1,0:T(8,128)(2,1)S(1)}, u32[]{:S(2)}, u32[]{:S(2)}) async-start(bf16[8,16,128]{2,1,0:T(8,128)(2,1)} %bitcast.9), calls=%async_computation.3 | async-start | bytes 65536 | tf_op jit(solution)/shard_map/all_to_all | solution.py:89
  69.3 22.0 %all-reduce = (f32[64]{0:T(128)S(1)}, f32[64]{0:T(128)S(1)}) all-reduce(f32[64]{0:T(128)S(1)} %get-tuple-element.36, f32[64]{0:T(128)S(1)} %get-tuple-element.35), channel_id=1, replica_groups=mesh['groups'=2,'wide'=8,'narrow'=2] {'wide'}, use_global_device_ids=true, to_apply=%region_10.15 | all-reduce | flops 128 | bytes 1024 | tf_op jit(solution)/shard_map/psum | solution.py:41
  92.2 55.0 %all-reduce.6.cloned.1.call-done = f32[4096,128]{1,0:T(8,128)} async-done(((f32[4096,128]{1,0:T(8,128)}), f32[4096,128]{1,0:T(8,128)}) %all-reduce.6.cloned.1.call-update) | async-done | bytes 2097168 | tf_op jit(solution)/shard_map/psum | solution.py:41
  147.2 1.8 divide_add_fusion.1
  149.8 1.4 copy-done.11
  151.2 0.8 fusion
  152.0 2.2 subtract_convert_fusion
  155.2 1.8 convolution_add_fusion
  157.1 1.5 copy-done.2
  158.6 1.3 fusion.8
  160.7 3.5 %all-reduce.1 = (f32[64,128]{1,0:T(8,128)S(1)}, f32[64]{0:T(128)S(1)}) all-reduce(f32[64,128]{1,0:T(8,128)S(1)} %convolution_add_fusion.2, f32[64]{0:T(128)S(1)} %get-tuple-element.25), channel_id=1, replica_groups=mesh['groups'=2,'wide'=8,'narrow'=2] {'narrow'}, use_global_device_ids=true, to_apply=%region_11.16 | all-reduce | flops 8256 | bytes 66048 | tf_op jit(solution)/shard_map/psum | solution.py:35
  165.7 3.9 %all-to-all-start.4 = ((bf16[8,16,128]{2,1,0:T(8,128)(2,1)}), bf16[8,16,128]{2,1,0:T(8,128)(2,1)S(1)}, u32[]{:S(2)}, u32[]{:S(2)}) async-start(bf16[8,16,128]{2,1,0:T(8,128)(2,1)} %bitcast.14), calls=%async_computation.4 | async-start | bytes 65536 | tf_op jit(solution)/shard_map/all_to_all | solution.py:97
  169.5 2.3 pad_maximum_fusion.2
  171.8 4.8 %all-to-all-done.4 = bf16[8,16,128]{2,1,0:T(8,128)(2,1)S(1)} async-done(((bf16[8,16,128]{2,1,0:T(8,128)(2,1)}), bf16[8,16,128]{2,1,0:T(8,128)(2,1)S(1)}, u32[]{:S(2)}, u32[]{:S(2)}) %all-to-all-start.4) | async-done | bytes 32800 | tf_op jit(solution)/shard_map/all_to_all | solution.py:97
  178.0 81.4 %all-reduce.8.cloned.1.call-done = f32[4096,128]{1,0:T(8,128)} async-done(((f32[4096,128]{1,0:T(8,128)}), f32[4096,128]{1,0:T(8,128)}) %all-reduce.8.cloned.1.call-update) | async-done | bytes 2097168 | tf_op jit(solution)/shard_map/psum | solution.py:41
  259.3 3.1 %divide_add_fusion = f32[4096,128]{1,0:T(8,128)} fusion(f32[4096,128]{1,0:T(8,128)S(1)} %copy-done.2, f32[4096,128]{1,0:T(8,128)} %all-reduce.8.cloned.1.call-done, f32[128]{0:T(128)S(1)} %maximum_add_fusion.3), kind=kLoop, calls=%fused_computation.22 | loop fusion | flops 1048576 | bytes 6291968 | tf_op jit(solution)/shard_map/add | solution.py:42
  (99 shorter events, 17.1 us)
Async XLA Ops:
  11.7 13.7 %all-to-all-start = ((s32[8,16,1]{1,2,0:T(1,128)}), s32[8,16,1]{1,2,0:T(1,128)S(1)}, u32[]{:S(2)}, u32[]{:S(2)}) async-start(s32[8,16,1]{1,2,0:T(1,128)} %bitcast.1), calls=%async_computation | async-start | bytes 8192 | tf_op jit(solution)/shard_map/all_to_all | solution.py:72
  19.1 4.0 %copy-start = (f32[4096,128]{1,0:T(8,128)S(1)}, f32[4096,128]{1,0:T(8,128)}, u32[]{:S(2)}) copy-start(f32[4096,128]{1,0:T(8,128)} %param.20) | copy-start | bytes 6291460
  23.0 0.8 copy-start.12
  23.0 0.8 copy-start.13
  23.0 0.8 copy-start.15
  26.9 14.9 %copy-start.14 = (f32[4096]{0:T(1024)S(1)}, f32[4096]{0:T(1024)}, u32[]{:S(2)}) copy-start(f32[4096]{0:T(1024)} %param.21) | copy-start | bytes 49156
  28.3 11.1 %all-to-all-start.1 = ((bf16[8,16,128]{2,1,0:T(8,128)(2,1)}), bf16[8,16,128]{2,1,0:T(8,128)(2,1)S(1)}, u32[]{:S(2)}, u32[]{:S(2)}) async-start(bf16[8,16,128]{2,1,0:T(8,128)(2,1)} %bitcast.4), calls=%async_computation.1 | async-start | bytes 65536 | tf_op jit(solution)/shard_map/all_to_all | solution.py:89
  32.7 114.6 %all-reduce.6.cloned.1.call-start = ((), (), s32[]{:S(2)}) async-start(), calls=%async_computation.5 | async-start | bytes 4194304 | tf_op jit(solution)/shard_map/psum | solution.py:41
  40.0 1.8 copy-start.5
  40.0 1.8 copy-start.10
  43.3 0.9 copy-start.9
  53.2 10.5 %all-to-all-start.2 = ((bf16[8,16,128]{2,1,0:T(8,128)(2,1)}), bf16[8,16,128]{2,1,0:T(8,128)(2,1)S(1)}, u32[]{:S(2)}, u32[]{:S(2)}) async-start(bf16[8,16,128]{2,1,0:T(8,128)(2,1)} %bitcast.7), calls=%async_computation.2 | async-start | bytes 65536 | tf_op jit(solution)/shard_map/all_to_all | solution.py:97
  65.8 25.6 %all-to-all-start.3 = ((bf16[8,16,128]{2,1,0:T(8,128)(2,1)}), bf16[8,16,128]{2,1,0:T(8,128)(2,1)S(1)}, u32[]{:S(2)}, u32[]{:S(2)}) async-start(bf16[8,16,128]{2,1,0:T(8,128)(2,1)} %bitcast.9), calls=%async_computation.3 | async-start | bytes 65536 | tf_op jit(solution)/shard_map/all_to_all | solution.py:89
  69.2 190.2 %all-reduce.8.cloned.1.call-start = ((), (), s32[]{:S(2)}) async-start(), calls=%async_computation.6 | async-start | bytes 4194304 | tf_op jit(solution)/shard_map/psum | solution.py:41
  149.0 3.0 %copy-start.1 = (f32[4096,128]{1,0:T(8,128)}, f32[4096,128]{1,0:T(8,128)S(1)}, u32[]{:S(2)}) copy-start(f32[4096,128]{1,0:T(8,128)S(1)} %divide_add_fusion.1) | copy-start | bytes 6291460
  149.2 2.0 copy-start.11
  149.8 4.4 %copy-start.3 = (bf16[4096,64]{1,0:T(8,128)(2,1)}, bf16[4096,64]{1,0:T(8,128)(2,1)S(1)}, u32[]{:S(2)}) copy-start(bf16[4096,64]{1,0:T(8,128)(2,1)S(1)} %get-tuple-element.26) | copy-start | bytes 1572868
  154.2 0.8 copy-start.6
  154.2 1.0 copy-start.8
  157.0 1.6 copy-start.2
  157.0 2.9 %copy-start.4 = (bf16[4096,64]{1,0:T(8,128)(2,1)S(1)}, bf16[4096,64]{1,0:T(8,128)(2,1)}, u32[]{:S(2)}) copy-start(bf16[4096,64]{1,0:T(8,128)(2,1)} %copy-done.3) | copy-start | bytes 1572868
  157.1 2.9 %copy-start.7 = (bf16[64,4096]{1,0:T(8,128)(2,1)S(1)}, bf16[64,4096]{1,0:T(8,128)(2,1)}, u32[]{:S(2)}) copy-start(bf16[64,4096]{1,0:T(8,128)(2,1)} %copy-done.6) | copy-start | bytes 1572868
  165.7 11.0 %all-to-all-start.4 = ((bf16[8,16,128]{2,1,0:T(8,128)(2,1)}), bf16[8,16,128]{2,1,0:T(8,128)(2,1)S(1)}, u32[]{:S(2)}, u32[]{:S(2)}) async-start(bf16[8,16,128]{2,1,0:T(8,128)(2,1)} %bitcast.14), calls=%async_computation.4 | async-start | bytes 65536 | tf_op jit(solution)/shard_map/all_to_all | solution.py:97
Sparse Core Ops, SparseCore 0:
  46.2 100.9 all-reduce.5
  157.2 102.1 all-reduce.7
where the time goes:
time: 270 us; the launch traced here: 269 us
  waiting for transfers between devices  156 us (58%)
  blocking collectives  28.9 us (11%)
  starting transfers between devices  22.3 us (8%)
  other arithmetic  18 us (7%)
  matrix products  15.3 us (6%)
  local copies, waits for them, and re-layouts  14.8 us (5%)
  between operations  14.4 us (5%)
    psum x2, waiting for transfers between devices, refine(): offset_grad, left_norm = lax.psum((offset_grad, left_norm), 'wide')  136 us
    psum x1, blocking collectives, refine(): offset_grad, left_norm = lax.psum((offset_grad, left_norm), 'wide')  22 us
    all_to_all x2, waiting for transfers between devices, local(): lax.all_to_all(outgoing.astype(jnp.bfloat16), 'wide', split_axis=0, conca...  12 us
    all_to_all x2, starting transfers between devices, local(): lax.all_to_all(answer, 'wide', split_axis=0, concat_axis=0, tiled=True)  7.71 us
    all_to_all x1, starting transfers between devices, local(): lax.all_to_all(request, 'wide', split_axis=0, concat_axis=0, tiled=True)  7.28 us
    all_to_all x2, starting transfers between devices, local(): lax.all_to_all(outgoing.astype(jnp.bfloat16), 'wide', split_axis=0, conca...  7.21 us
    psum x2, blocking collectives, refine(): row_grad, right_norm = lax.psum((row_grad, right_norm), 'narrow')  6.91 us
    all_to_all x2, waiting for transfers between devices, local(): lax.all_to_all(answer, 'wide', split_axis=0, concat_axis=0, tiled=True)  5.54 us
  transfers between devices with their start and end apart: 7, of which 6 were waited for; matrix products, arithmetic and copies ran while one was open for 7% of the time, Pallas kernels for 0%

commit v1 on v0

v1 whole, which is shorter than its diff:
```python
from functools import partial

import jax
import jax.numpy as jnp
from jax import lax
from jax.experimental import pallas as pl
from jax.experimental.pallas import tpu as pltpu
from jax.sharding import PartitionSpec as P

epsilon = 1e-06
F32 = jnp.float32
BF16 = jnp.bfloat16


def turned(rows):
    half = rows.shape[1] // 2
    return jnp.concatenate([rows[:, half:], -rows[:, :half]], 1)


def unturned(rows):
    half = rows.shape[1] // 2
    return jnp.concatenate([-rows[:, half:], rows[:, :half]], 1)


def both_halves(norm):
    half = norm.shape[1] // 2
    once = norm[:, :half] + norm[:, half:]
    return jnp.concatenate([once, once], 1)


def residual_of(piece, model, inside, level):
    rows = inside.shape[0]
    real = jnp.where(inside, piece[0].astype(F32) - model[:rows], 0.0)
    imag = jnp.where(inside, piece[1].astype(F32) - model[rows:], 0.0)
    kept = level * lax.rsqrt(jnp.maximum(real * real + imag * imag, level * level))
    return real, imag, kept


def live_mask(begin, end, first_col, count):
    column = first_col + lax.broadcasted_iota(jnp.int32, (begin.shape[0], count), 1)
    return (column >= begin) & (column < end)


def rows_body(base_ref, piece_ref, left_ref, right_ref, level_ref, begin_ref, end_ref, grad_ref, norm_ref, acc_ref):
    step = pl.program_id(0)
    rows = left_ref.shape[0]
    cols = right_ref.shape[0]

    @pl.when(step == 0)
    def _():
        acc_ref[...] = jnp.zeros_like(acc_ref)
        norm_ref[...] = jnp.zeros_like(norm_ref)

    low = left_ref[...].astype(BF16)
    pair = jnp.concatenate([low, turned(low)], 0)
    right = right_ref[...]
    right_low = right.astype(BF16)
    model = lax.dot_general(pair, right_low, (((1,), (1,)), ((), ())), preferred_element_type=F32)
    inside = live_mask(begin_ref[...], end_ref[...], base_ref[0] + step * cols, cols)
    real, imag, kept = residual_of(piece_ref, model, inside, level_ref[...])
    error = jnp.concatenate([(real * kept).astype(BF16), (imag * kept).astype(BF16)], 0)
    acc_ref[...] += jnp.dot(error, right_low, preferred_element_type=F32)
    norm_ref[...] += jnp.sum(right * right, 0, keepdims=True)

    @pl.when(step == pl.num_programs(0) - 1)
    def _():
        grad_ref[...] = acc_ref[:rows] + unturned(acc_ref[rows:])


def cols_body(with_step, base_ref, piece_ref, left_ref, *refs):
    if with_step:
        move_ref, right_ref, level_ref, begin_ref, end_ref, next_ref, norm_ref, part_ref, acc_ref, left_norm_ref = refs
    else:
        right_ref, level_ref, begin_ref, end_ref, next_ref, norm_ref, acc_ref, left_norm_ref = refs
    step = pl.program_id(0)
    rows = left_ref.shape[0]
    cols = right_ref.shape[0]

    @pl.when(step == 0)
    def _():
        acc_ref[...] = jnp.zeros_like(acc_ref)
        left_norm_ref[...] = jnp.zeros_like(left_norm_ref)

    left = left_ref[...]
    if with_step:
        left = left + move_ref[...].astype(F32)
    low = left.astype(BF16)
    pair = jnp.concatenate([low, turned(low)], 0)
    right_low = right_ref[...].astype(BF16)
    model = lax.dot_general(pair, right_low, (((1,), (1,)), ((), ())), preferred_element_type=F32)
    inside = live_mask(begin_ref[...], end_ref[...], base_ref[0], cols)
    real, imag, kept = residual_of(piece_ref, model, inside, level_ref[...])
    error = jnp.concatenate([(real * kept).astype(BF16), (imag * kept).astype(BF16)], 0)
    acc_ref[...] += lax.dot_general(pair, error, (((0,), (0,)), ((), ())), preferred_element_type=F32)
    left_norm_ref[...] += jnp.sum(left * left, 0, keepdims=True)
    if with_step:
        part = jnp.dot(error, right_low, preferred_element_type=F32)
        part_ref[...] = part[:rows] + unturned(part[rows:])

    @pl.when(step == pl.num_programs(0) - 1)
    def _():
        right = right_ref[...]
        norm_ref[...] = jnp.sum(right * right, 0, keepdims=True)
        next_ref[...] = right + acc_ref[...].T / (both_halves(left_norm_ref[...]) + epsilon)


def sparse_body(base_ref, piece_ref, left_ref, right_ref, level_ref, begin_ref, end_ref, out_ref):
    step = pl.program_id(0)
    cols = right_ref.shape[0]
    low = left_ref[...].astype(BF16)
    pair = jnp.concatenate([low, turned(low)], 0)
    model = lax.dot_general(pair, right_ref[...], (((1,), (1,)), ((), ())), preferred_element_type=F32)
    inside = live_mask(begin_ref[...], end_ref[...], base_ref[0] + step * cols, cols)
    real, imag, kept = residual_of(piece_ref, model, inside, level_ref[...])
    out_ref[0] = (real - real * kept).astype(BF16)
    out_ref[1] = (imag - imag * kept).astype(BF16)


def col_block(count):
    block = min(512, count)
    while count % block:
        block //= 2
    return block


def whole(shape):
    return pl.BlockSpec(shape, lambda i, base: (0,) * len(shape))


def row_pass(base, pieces, left, right, level, begin, end):
    _, rows, cols = pieces.shape
    width = right.shape[1]
    block = col_block(cols)
    return pl.pallas_call(
        rows_body,
        grid_spec=pltpu.PrefetchScalarGridSpec(
            num_scalar_prefetch=1,
            grid=(cols // block,),
            in_specs=[
                pl.BlockSpec((2, rows, block), lambda i, base: (0, 0, i)),
                whole((rows, width)),
                pl.BlockSpec((block, width), lambda i, base: (i, 0)),
                pl.BlockSpec((1, block), lambda i, base: (0, i)),
                whole((rows, 1)),
                whole((rows, 1)),
            ],
            out_specs=[whole((rows, width)), whole((1, width))],
            scratch_shapes=[pltpu.VMEM((2 * rows, width), F32)],
        ),
        out_shape=[jax.ShapeDtypeStruct((rows, width), F32), jax.ShapeDtypeStruct((1, width), F32)],
        name="row_pass",
    )(base, pieces, left, right, level, begin, end)


def col_pass(base, turned_pieces, left, move, right, level, begin, end):
    count, _, rows, cols = turned_pieces.shape
    width = right.shape[1]
    by_block = pl.BlockSpec((rows, width), lambda i, base: (i, 0))
    ends = pl.BlockSpec((rows, 1), lambda i, base: (i, 0))
    with_step = move is not None
    return pl.pallas_call(
        partial(cols_body, with_step),
        grid_spec=pltpu.PrefetchScalarGridSpec(
            num_scalar_prefetch=1,
            grid=(count,),
            in_specs=[pl.BlockSpec((None, 2, rows, cols), lambda i, base: (i, 0, 0, 0)), by_block]
            + [by_block] * with_step
            + [whole((cols, width)), whole((1, cols)), ends, ends],
            out_specs=[whole((cols, width)), whole((1, width))] + [by_block] * with_step,
            scratch_shapes=[pltpu.VMEM((width, cols), F32), pltpu.VMEM((1, width), F32)],
        ),
        out_shape=[jax.ShapeDtypeStruct((cols, width), F32), jax.ShapeDtypeStruct((1, width), F32)]
        + [jax.ShapeDtypeStruct((count * rows, width), F32)] * with_step,
        name="col_pass_2" if with_step else "col_pass_1",
    )(base, turned_pieces, left, *([move] if with_step else []), right, level, begin, end)


def sparse_pass(base, pieces, left, right, level, begin, end):
    _, rows, cols = pieces.shape
    width = right.shape[1]
    block = col_block(cols)
    tall = pl.BlockSpec((2, rows, block), lambda i, base: (0, 0, i))
    return pl.pallas_call(
        sparse_body,
        grid_spec=pltpu.PrefetchScalarGridSpec(
            num_scalar_prefetch=1,
            grid=(cols // block,),
            in_specs=[
                tall,
                whole((rows, width)),
                pl.BlockSpec((block, width), lambda i, base: (i, 0)),
                pl.BlockSpec((1, block), lambda i, base: (0, i)),
                whole((rows, 1)),
                whole((rows, 1)),
            ],
            out_specs=tall,
        ),
        out_shape=jax.ShapeDtypeStruct(pieces.shape, BF16),
        name="sparse_pass",
    )(base, pieces, left, right, level, begin, end)


def exchange(blocks):
    return lax.all_to_all(blocks, "wide", split_axis=0, concat_axis=0, tiled=True)


def gather(block):
    return exchange(jnp.broadcast_to(block[None], (lax.axis_size("wide"),) + block.shape))


def swap_narrow(value):
    count = lax.axis_size("narrow")
    total = value
    for shift in range(1, count):
        total = total + lax.ppermute(value, "narrow", [(i, (i + shift) % count) for i in range(count)])
    return total


def as_rows(values, width):
    rows = -(-values.shape[0] // (8 * width)) * 8
    return jnp.pad(values, (0, rows * width - values.shape[0])).reshape(rows, width)


def local(pieces, destination, first_offset, valid_length, midpoint_factor, offset_factor, threshold):
    count = lax.axis_size("wide")
    _, rows, cols = pieces.shape
    width = offset_factor.shape[1]
    part = cols // count
    me = lax.axis_index("wide")
    base = lax.axis_index("narrow") * cols
    base_all = jnp.full((1,), base, jnp.int32)
    base_part = jnp.full((1,), base + me * part, jnp.int32)
    level = threshold[None, :]

    numbers = jnp.concatenate([destination, first_offset, first_offset + valid_length]).astype(F32)
    header = jnp.concatenate([midpoint_factor, as_rows(numbers, width)], 0)
    headers = gather(header)
    blocks = exchange(jnp.transpose(pieces.reshape(2, rows, count, part), (2, 0, 1, 3)))

    all_rows = headers[:, :rows].reshape(count * rows, width)
    tables = headers[:, rows:].reshape(count, -1)[:, : 3 * rows].astype(jnp.int32).reshape(count, 3, rows)
    dest_all = tables[:, 0].reshape(-1)
    begin_all = tables[:, 1].reshape(-1, 1)
    end_all = tables[:, 2].reshape(-1, 1)
    left_all = jnp.take(all_rows, dest_all, axis=0)
    left_mine = lax.dynamic_slice_in_dim(left_all, me * rows, rows, 0)
    begin = first_offset[:, None]
    end = begin + valid_length[:, None]

    grad, norm = row_pass(base_all, pieces, left_mine, offset_factor, level, begin, end)
    summed = swap_narrow(jnp.concatenate([grad, jnp.broadcast_to(norm, (8, width))], 0))
    move_mine = (summed[:rows] / (both_halves(summed[rows : rows + 1]) + epsilon)).astype(BF16)
    move_all = gather(move_mine).reshape(count * rows, width)

    right_part = lax.dynamic_slice_in_dim(offset_factor, me * part, part, 0)
    level_part = lax.dynamic_slice_in_dim(level, me * part, part, 1)
    right_one, _ = col_pass(base_part, blocks, left_all, None, right_part, level_part, begin_all, end_all)
    right_low = right_one.astype(BF16)
    low_all = gather(right_low).reshape(cols, width)

    right_two, norm_one, row_part = col_pass(
        base_part, blocks, left_all, move_all, right_one, level_part, begin_all, end_all
    )
    change_all = gather((right_two - right_low.astype(F32)).astype(BF16)).reshape(cols, width)

    segment_of = jnp.sum(
        jnp.where(
            dest_all[None, :] == jnp.arange(count * rows, dtype=jnp.int32)[:, None],
            jnp.arange(count * rows, dtype=jnp.int32)[None, :],
            0,
        ),
        1,
    )
    norm_high = norm_one.astype(BF16)
    norm_low = (norm_one - norm_high.astype(F32)).astype(BF16)
    norm_rows = jnp.concatenate([norm_high, norm_low, jnp.zeros((6, width), BF16)], 0)
    outgoing = jnp.concatenate(
        [
            jnp.take(row_part, segment_of, axis=0).astype(BF16).reshape(count, rows, width),
            jnp.broadcast_to(norm_rows[None], (count,) + norm_rows.shape),
        ],
        1,
    )
    summed = swap_narrow(jnp.sum(exchange(outgoing).astype(F32), 0))
    norm_two = both_halves(summed[rows : rows + 1] + summed[rows + 1 : rows + 2])
    my_segments = lax.dynamic_slice_in_dim(segment_of, me * rows, rows, 0)
    new_midpoint = (
        midpoint_factor + jnp.take(move_all, my_segments, axis=0).astype(F32) + summed[:rows] / (norm_two + epsilon)
    )

    left_mine = left_mine + move_mine.astype(F32)
    sparse = sparse_pass(base_all, pieces, left_mine, low_all, level, begin, end)
    new_offset = low_all.astype(F32) + change_all.astype(F32)
    return sparse, new_midpoint, new_offset


def solution(mesh):
    placed = (
        P(None, ("groups", "wide"), "narrow"),
        P("wide"),
        P("wide"),
        P("wide"),
        P(("groups", "wide"), None),
        P(("groups", "narrow"), None),
        P(("groups", "narrow")),
    )
    return jax.shard_map(
        local,
        mesh=mesh,
        in_specs=placed,
        out_specs=(
            P(None, ("groups", "wide"), "narrow"),
            P(("groups", "wide"), None),
            P(("groups", "narrow"), None),
        ),
        check_vma=False,
    )
```

time: 270 us -> 149 us (0.55)
  waiting for transfers between devices: 156 us -> 40 us
  Pallas kernels: 0 us -> 28.5 us
  matrix products: 15.3 us -> 0 us
  between operations: 14.4 us -> 0.83 us
  other arithmetic: 18 us -> 9.14 us
  local copies, waits for them, and re-layouts: 14.8 us -> 17.8 us
    psum x2 -> x0, waiting for transfers between devices: 136 us -> none  [refine(): offset_grad, left_norm = lax.psum((offset_grad, left_norm), 'wide')]
    psum x3 -> x0, blocking collectives: 28.9 us -> none  [the longest x1 22 us: refine(): offset_grad, left_norm = lax.psum((offset_grad, left_norm), 'wide')]
    pallas_call x0 -> x4, Pallas kernels: none -> 28.5 us  [the longest x2 15.1 us: col_pass(): pl.pallas_call(partial(cols_body, with_step), grid_spec=pltpu.PrefetchSca...]
    all_to_all x0 -> x1, blocking collectives: none -> 27.4 us  [exchange(): lax.all_to_all(blocks, 'wide', split_axis=0, concat_axis=0, tiled=True)]
    all_to_all x5, waiting for transfers between devices: 19.2 us -> 38.4 us  [exchange(): lax.all_to_all(blocks, 'wide', split_axis=0, concat_axis=0, tiled=True)]
    dot_general x12 -> x0, matrix products: 15.3 us -> none  [the longest x2 3.87 us: refine(): jnp.dot(row_factor, right_low.T, preferred_element_type=jnp.float32)]
    broadcast_in_dim x1 -> x8, local copies, waits for them, and re-layouts: 0.01 us -> 4.7 us  [the longest x4 2.68 us: gather(): jnp.broadcast_to(block[None], (lax.axis_size('wide'),) + block.shape)]
    reduce_sum x4 -> x2, other arithmetic: 4.85 us -> 0.21 us  [the longest x1 0.19 us: local(): jnp.sum(jnp.where(dest_all[None, :] == jnp.arange(count * rows, dtype=jnp...]
  transfers between devices with their start and end apart: 7 -> 7, of which waited for: 6 -> 6; matrix products, arithmetic and copies ran while one was open for 7% -> 11% of each run, Pallas kernels for 0% -> 14%
where the time goes in v1:
time: 149 us; the launch traced here: 148 us
  waiting for transfers between devices  40 us (27%)
  Pallas kernels  28.5 us (19%)
  blocking collectives  27.4 us (18%)
  starting transfers between devices  24.1 us (16%)
  local copies, waits for them, and re-layouts  17.8 us (12%)
  other arithmetic  9.14 us (6%)
    all_to_all x5, waiting for transfers between devices, exchange(): lax.all_to_all(blocks, 'wide', split_axis=0, concat_axis=0, tiled=True)  38.4 us
    all_to_all x1, blocking collectives, exchange(): lax.all_to_all(blocks, 'wide', split_axis=0, concat_axis=0, tiled=True)  27.4 us
    all_to_all x5, starting transfers between devices, exchange(): lax.all_to_all(blocks, 'wide', split_axis=0, concat_axis=0, tiled=True)  24 us
    pallas_call x2, Pallas kernels, col_pass(): pl.pallas_call(partial(cols_body, with_step), grid_spec=pltpu.PrefetchSca...  15.1 us
    pallas_call x1, Pallas kernels, row_pass(): pl.pallas_call(rows_body, grid_spec=pltpu.PrefetchScalarGridSpec(num_scal...  6.87 us
    pallas_call x1, Pallas kernels, sparse_pass(): pl.pallas_call(sparse_body, grid_spec=pltpu.PrefetchScalarGridSpec(num_sc...  6.52 us
  transfers between devices with their start and end apart: 7, of which 6 were waited for; matrix products, arithmetic and copies ran while one was open for 11% of the time, Pallas kernels for 14%

profile of v1, /device:TPU:0, one launch (start us, length us, event | category | flops | bytes accessed | tf_op | source)
XLA Modules:
  0.0 147.7 jit_solution(5670000809349523505)
XLA Ops:
  1.3 0.7 add_convert_fusion
  2.1 0.8 pad_maximum_fusion.1
  2.8 0.7 broadcast_in_dim.89
  3.6 7.3 %all-to-all-start = ((f32[8,72,128]{2,1,0:T(8,128)}), f32[8,72,128]{2,1,0:T(8,128)S(1)}, u32[]{:S(2)}, u32[]{:S(2)}) async-start(f32[8,72,128]{2,1,0:T(8,128)} %broadcast_in_dim.89), calls=%async_computation | async-start | bytes 589824 | tf_op jit(solution)/shard_map/all_to_all | solution.py:204
  11.5 1.3 copy.23.begin_ref
  12.9 2.3 %copy.36 = bf16[2,8,8,8,512]{4,3,1,0,2:T(8,128)(2,1)} copy(bf16[2,8,8,8,512]{4,3,2,1,0:T(8,128)(2,1)} %bitcast.34) | data formatting | bytes 2097152 | tf_op jit(solution)/shard_map/reshape | solution.py:238
  15.2 1.3 dynamic-slice.3
  16.6 1.7 %constant_dynamic-slice_fusion.refs_0_ = f32[512,128]{1,0:T(8,128)} fusion(f32[4096,128]{1,0:T(8,128)} %right_ref.1, s32[]{:T(128)S(6)} %select_n.29), kind=kLoop, calls=%fused_computation.44 | loop fusion | bytes 524292 | tf_op jit(solution)/shard_map/dynamic_slice | solution.py:255
  18.3 2.2 %all-to-all-done = f32[8,72,128]{2,1,0:T(8,128)S(1)} async-done(((f32[8,72,128]{2,1,0:T(8,128)}), f32[8,72,128]{2,1,0:T(8,128)S(1)}, u32[]{:S(2)}, u32[]{:S(2)}) %all-to-all-start) | async-done | bytes 294944 | tf_op jit(solution)/shard_map/all_to_all | solution.py:204
  20.5 3.8 %all-to-all-start.1 = ((bf16[8,2,64,512]{3,2,1,0:T(8,128)(2,1)}), bf16[8,2,64,512]{3,2,1,0:T(8,128)(2,1)S(1)}, u32[]{:S(2)}, u32[]{:S(2)}) async-start(bf16[8,2,64,512]{3,2,1,0:T(8,128)(2,1)} %bitcast.31), calls=%async_computation.1 | async-start | bytes 2097152 | tf_op jit(solution)/shard_map/all_to_all | solution.py:204
  24.5 1.0 gather_fusion.1
  26.4 6.9 %row_pass.1 = (f32[64,128]{1,0:T(8,128)}, f32[1,128]{1,0:T(1,128)}) custom-call(s32[1]{0:T(128)} %bitcast.base_ref, bf16[2,64,4096]{2,1,0:T(8,128)(2,1)} %piece_ref.3, f32[64,128]{1,0:T(8,128)} %constant_dynamic-slice_fusion.1.left_ref, f32[4096,128]{1,0:T(8,128)} %right_ref.1, f32[1,4096]{1,0:T(1,128)} %bitcast.39, s32[64,1]{1,0:T(8,128)} %copy.23.begin_ref, ...), custom_call_target="tpu_custom_call" | custom-call | tf_op jit(solution)/shard_map/row_pass/pallas_call | solution.py:134
  34.0 0.8 pad_maximum_fusion.2
  34.9 1.0 collective-permute-done
  35.9 0.8 fusion.3
  37.5 12.2 %all-to-all-done.1.piece_ref = bf16[8,2,64,512]{3,2,1,0:T(8,128)(2,1)S(1)} async-done(((bf16[8,2,64,512]{3,2,1,0:T(8,128)(2,1)}), bf16[8,2,64,512]{3,2,1,0:T(8,128)(2,1)S(1)}, u32[]{:S(2)}, u32[]{:S(2)}) %all-to-all-start.1) | async-done | bytes 1048608 | tf_op jit(solution)/shard_map/all_to_all | solution.py:204
  49.7 0.7 broadcast_in_dim.99
  50.4 3.4 %all-to-all-start.3 = ((bf16[8,64,128]{2,1,0:T(8,128)(2,1)}), bf16[8,64,128]{2,1,0:T(8,128)(2,1)S(1)}, u32[]{:S(2)}, u32[]{:S(2)}) async-start(bf16[8,64,128]{2,1,0:T(8,128)(2,1)} %broadcast_in_dim.99), calls=%async_computation.3 | async-start | bytes 262144 | tf_op jit(solution)/shard_map/all_to_all | solution.py:204
  53.8 0.9 reshape_squeeze.12.refs_2_.refs_3_
  54.7 0.9 reshape_squeeze.13.refs_3_.refs_4_
  55.6 7.1 %col_pass_1.1 = (f32[512,128]{1,0:T(8,128)}, f32[1,128]{1,0:T(1,128)}) custom-call(s32[1]{0:T(128)} %bitcast.8.base_ref, bf16[8,2,64,512]{3,2,1,0:T(8,128)(2,1)} %copy-done, f32[512,128]{1,0:T(8,128)} %copy-done.2, f32[512,128]{1,0:T(8,128)} %constant_dynamic-slice_fusion.refs_0_, f32[1,512]{1,0:T(1,128)} %bitcast.42, ...), custom_call_target="tpu_custom_call" | custom-call | tf_op jit(solution)/shard_map/col_pass_1/pallas_call | solution.py:161
  63.4 7.9 %col_pass_2.1 = (f32[512,128]{1,0:T(8,128)}, f32[1,128]{1,0:T(1,128)}, f32[512,128]{1,0:T(8,128)}) custom-call(s32[1]{0:T(128)} %bitcast.8.base_ref, bf16[8,2,64,512]{3,2,1,0:T(8,128)(2,1)} %copy-done, f32[512,128]{1,0:T(8,128)} %copy-done.2, bf16[512,128]{1,0:T(8,128)(2,1)} %bitcast.36, f32[512,128]{1,0:T(8,128)} %get-tuple-element.12.refs_1_, ...), custom_call_target="tpu_custom_call" | custom-call | tf_op jit(solution)/shard_map/col_pass_2/pallas_call | solution.py:161
  71.4 0.7 fusion.5
  72.1 2.0 %gather_fusion.2 = bf16[512,128]{1,0:T(8,128)(2,1)S(1)} fusion(f32[512,128]{1,0:T(8,128)} %get-tuple-element.13, s32[1024]{0:T(1024)S(1)} %pad_clamp_fusion), kind=kCustom, calls=%fused_computation.1.clone | custom fusion | bytes 264192 | tf_op jit(solution)/shard_map/jit(_take)/gather | solution.py:279
  75.0 6.0 %all-to-all-start.4 = ((bf16[8,72,128]{2,1,0:T(8,128)(2,1)}), bf16[8,72,128]{2,1,0:T(8,128)(2,1)S(1)}, u32[]{:S(2)}, u32[]{:S(2)}) async-start(bf16[8,72,128]{2,1,0:T(8,128)(2,1)} %pad_maximum_fusion), calls=%async_computation.4 | async-start | bytes 294912 | tf_op jit(solution)/shard_map/all_to_all | solution.py:204
  81.0 7.4 %all-to-all-done.4 = bf16[8,72,128]{2,1,0:T(8,128)(2,1)S(1)} async-done(((bf16[8,72,128]{2,1,0:T(8,128)(2,1)}), bf16[8,72,128]{2,1,0:T(8,128)(2,1)S(1)}, u32[]{:S(2)}, u32[]{:S(2)}) %all-to-all-start.4) | async-done | bytes 147488 | tf_op jit(solution)/shard_map/all_to_all | solution.py:204
  88.6 27.4 %all_to_all.30 = bf16[8,512,128]{2,1,0:T(8,128)(2,1)} all-to-all(bf16[8,512,128]{2,1,0:T(8,128)(2,1)S(1)} %broadcast_in_dim.95), channel_id=1, replica_groups=mesh['groups'=2,'wide'=8,'narrow'=2] {'wide'}, dimensions={0} | all-to-all | bytes 2097152 | tf_op jit(solution)/shard_map/all_to_all | solution.py:204
  115.9 1.1 broadcast_in_dim.104
  117.0 3.6 %all-to-all-start.5 = ((bf16[8,512,128]{2,1,0:T(8,128)(2,1)}), bf16[8,512,128]{2,1,0:T(8,128)(2,1)S(1)}, u32[]{:S(2)}, u32[]{:S(2)}) async-start(bf16[8,512,128]{2,1,0:T(8,128)(2,1)} %broadcast_in_dim.104), calls=%async_computation.5 | async-start | bytes 2097152 | tf_op jit(solution)/shard_map/all_to_all | solution.py:204
  122.9 6.5 %sparse_pass.1 = bf16[2,64,4096]{2,1,0:T(8,128)(2,1)} custom-call(s32[1]{0:T(128)} %bitcast.base_ref, bf16[2,64,4096]{2,1,0:T(8,128)(2,1)} %piece_ref.3, f32[64,128]{1,0:T(8,128)} %get-tuple-element.23.left_ref, bf16[4096,128]{1,0:T(8,128)(2,1)} %bitcast.35, f32[1,4096]{1,0:T(1,128)} %bitcast.40, s32[64,1]{1,0:T(8,128)} %copy.23.begin_ref, s32[64,1]{1,0:T(8,128)} %copy.24.end_ref), custom_call_target="tpu_custom_call" | custom-call | tf_op jit(solution)/shard_map/sparse_pass/pallas_call | solution.py:183
  129.4 16.6 %all-to-all-done.5 = bf16[8,512,128]{2,1,0:T(8,128)(2,1)S(1)} async-done(((bf16[8,512,128]{2,1,0:T(8,128)(2,1)}), bf16[8,512,128]{2,1,0:T(8,128)(2,1)S(1)}, u32[]{:S(2)}, u32[]{:S(2)}) %all-to-all-start.5) | async-done | bytes 1048608 | tf_op jit(solution)/shard_map/all_to_all | solution.py:204
  146.1 1.7 %convert_add_fusion = f32[4096,128]{1,0:T(8,128)} fusion(bf16[8,512,128]{2,1,0:T(8,128)(2,1)S(1)} %all-to-all-done.5, bf16[8,512,128]{2,1,0:T(8,128)(2,1)S(1)} %copy-done.1), kind=kLoop, calls=%fused_computation.3 | loop fusion | flops 1572864 | bytes 4194304 | tf_op jit(solution)/shard_map/add | solution.py:293
  (60 shorter events, 8.1 us)
Async XLA Ops:
  3.6 16.9 %all-to-all-start = ((f32[8,72,128]{2,1,0:T(8,128)}), f32[8,72,128]{2,1,0:T(8,128)S(1)}, u32[]{:S(2)}, u32[]{:S(2)}) async-start(f32[8,72,128]{2,1,0:T(8,128)} %broadcast_in_dim.89), calls=%async_computation | async-start | bytes 589824 | tf_op jit(solution)/shard_map/all_to_all | solution.py:204
  20.5 29.2 %all-to-all-start.1 = ((bf16[8,2,64,512]{3,2,1,0:T(8,128)(2,1)}), bf16[8,2,64,512]{3,2,1,0:T(8,128)(2,1)S(1)}, u32[]{:S(2)}, u32[]{:S(2)}) async-start(bf16[8,2,64,512]{3,2,1,0:T(8,128)(2,1)} %bitcast.31), calls=%async_computation.1 | async-start | bytes 2097152 | tf_op jit(solution)/shard_map/all_to_all | solution.py:204
  25.7 29.0 %copy-start.2 = (f32[512,128]{1,0:T(8,128)}, f32[512,128]{1,0:T(8,128)S(1)}, u32[]{:S(2)}) copy-start(f32[512,128]{1,0:T(8,128)S(1)} %broadcast_select_fusion.left_ref) | copy-start | bytes 786436
  34.7 1.2 collective-permute-start
  49.7 5.9 %copy-start = (bf16[8,2,64,512]{3,2,1,0:T(8,128)(2,1)}, bf16[8,2,64,512]{3,2,1,0:T(8,128)(2,1)S(1)}, u32[]{:S(2)}) copy-start(bf16[8,2,64,512]{3,2,1,0:T(8,128)(2,1)S(1)} %all-to-all-done.1.piece_ref) | copy-start | bytes 3145732
  50.4 12.4 %all-to-all-start.3 = ((bf16[8,64,128]{2,1,0:T(8,128)(2,1)}), bf16[8,64,128]{2,1,0:T(8,128)(2,1)S(1)}, u32[]{:S(2)}, u32[]{:S(2)}) async-start(bf16[8,64,128]{2,1,0:T(8,128)(2,1)} %broadcast_in_dim.99), calls=%async_computation.3 | async-start | bytes 262144 | tf_op jit(solution)/shard_map/all_to_all | solution.py:204
  62.8 0.6 copy-start.3
  63.4 17.6 %copy-start.5 = (f32[512,128]{1,0:T(8,128)S(1)}, f32[512,128]{1,0:T(8,128)}, u32[]{:S(2)}) copy-start(f32[512,128]{1,0:T(8,128)} %get-tuple-element.12.refs_1_) | copy-start | bytes 786436
  71.3 9.6 %copy-start.6 = (f32[512,128]{1,0:T(8,128)S(1)}, f32[512,128]{1,0:T(8,128)}, u32[]{:S(2)}) copy-start(f32[512,128]{1,0:T(8,128)} %get-tuple-element.15) | copy-start | bytes 786436
  75.0 13.4 %all-to-all-start.4 = ((bf16[8,72,128]{2,1,0:T(8,128)(2,1)}), bf16[8,72,128]{2,1,0:T(8,128)(2,1)S(1)}, u32[]{:S(2)}, u32[]{:S(2)}) async-start(bf16[8,72,128]{2,1,0:T(8,128)(2,1)} %pad_maximum_fusion), calls=%async_computation.4 | async-start | bytes 294912 | tf_op jit(solution)/shard_map/all_to_all | solution.py:204
  115.9 4.9 %copy-start.4 = (bf16[8,64,128]{2,1,0:T(8,128)(2,1)S(1)}, bf16[8,64,128]{2,1,0:T(8,128)(2,1)}, u32[]{:S(2)}) copy-start(bf16[8,64,128]{2,1,0:T(8,128)(2,1)} %copy-done.3) | copy-start | bytes 393220
  115.9 6.3 %copy-start.7 = (f32[64,128]{1,0:T(8,128)S(1)}, f32[64,128]{1,0:T(8,128)}, u32[]{:S(2)}) copy-start(f32[64,128]{1,0:T(8,128)} %param.13) | copy-start | bytes 98308
  117.0 29.0 %all-to-all-start.5 = ((bf16[8,512,128]{2,1,0:T(8,128)(2,1)}), bf16[8,512,128]{2,1,0:T(8,128)(2,1)S(1)}, u32[]{:S(2)}, u32[]{:S(2)}) async-start(bf16[8,512,128]{2,1,0:T(8,128)(2,1)} %broadcast_in_dim.104), calls=%async_computation.5 | async-start | bytes 2097152 | tf_op jit(solution)/shard_map/all_to_all | solution.py:204
  120.6 25.4 %copy-start.1 = (bf16[8,512,128]{2,1,0:T(8,128)(2,1)S(1)}, bf16[8,512,128]{2,1,0:T(8,128)(2,1)}, u32[]{:S(2)}) copy-start(bf16[8,512,128]{2,1,0:T(8,128)(2,1)} %all_to_all.30) | copy-start | bytes 3145732
  120.7 1.3 collective-permute-start.1
